TPU v7x, 128 devices: a whole 4x4x4 slice. The times are simulated.
128 devices in a mesh: row: 8 (over x, y_lo), col: 8 (over z, y_hi), depth: 2 (over core).
Axes of the slice: x: 4, y: 4 (y_hi: 2, y_lo: 2; y = y_hi * 2 + y_lo), z: 4, core: 2. Of those that a mesh axis runs over, the one named last changes fastest.
Arguments:
- amplitudes: bfloat16 [20480, 20480], P('row', 'col'), may hold values from -0.109375 to 0.109375
- coulomb_vertex: bfloat16 [256, 20480], P('depth', ('row', 'col')), may hold values from -1.5 to 1.5
Outputs:
- cycle_residual: bfloat16 [20480, 20480], P('row', ('col', 'depth'))
- structure_factor: float32 [256], P('depth')
All inputs are finite; a program needn't handle non-finite values.
Results may differ from a plain program's by a relative error of at most 0.0057.
Values may be sent and summed in bfloat16 or wider, within the bound.
No kernel may reach another device: no remote copies, remote signals or barrier semaphores. Data moves between devices by JAX's collectives and lax.ppermute only.
A program may use at most 128 MiB of HBM per device.

v0:
```python
import jax
import jax.numpy as jnp
from jax import lax
from jax.sharding import PartitionSpec as P


def broadcast(array, axis, root):
    mine = lax.axis_index(axis) == root
    return lax.psum(jnp.where(mine, array, jnp.zeros_like(array)), axis)


def body(amplitudes, coulomb_vertex):
    row_index = lax.axis_index("row")
    col_index = lax.axis_index("col")
    block_width = amplitudes.shape[0]
    on_diagonal = (row_index == col_index).astype(jnp.float32)
    vertex_rows = lax.all_gather(coulomb_vertex, "col", axis=1, tiled=True)
    vertex_cols = broadcast(vertex_rows, "row", col_index)
    dressing = jnp.dot(vertex_rows, amplitudes, preferred_element_type=jnp.float32)
    factor_part = jnp.sum(dressing * vertex_cols.astype(jnp.float32), axis=1)
    structure_factor = lax.psum(factor_part, ("row", "col"))
    dressed_term = dressing + on_diagonal * vertex_rows.astype(jnp.float32)
    dressed_part = lax.psum_scatter(dressed_term, "row", scatter_dimension=1, tiled=True)
    dressed = dressed_part.astype(jnp.bfloat16)
    everything = lax.all_gather(dressed, ("row", "col"), axis=1, tiled=True)
    fields_here = everything.shape[0]
    grid_side = lax.axis_size("row")
    ordered = everything.reshape(fields_here, grid_side, grid_side, dressed.shape[1])
    ordered = jnp.transpose(ordered, (0, 2, 1, 3)).reshape(
        fields_here, grid_side * grid_side * dressed.shape[1]
    )
    dressed_cols = lax.dynamic_slice_in_dim(ordered, col_index * block_width, block_width, 1)
    dressed_rows = lax.dynamic_slice_in_dim(ordered, row_index * block_width, block_width, 1)
    cols_all = lax.all_to_all(dressed_cols, "depth", split_axis=1, concat_axis=0, tiled=True)
    rows_all = lax.all_gather(dressed_rows, "depth", axis=0, tiled=True)
    product = lax.dot_general(
        rows_all, cols_all, (((0,), (0,)), ((), ())), preferred_element_type=jnp.float32
    )
    cycle_residual = product.astype(jnp.bfloat16)
    return (cycle_residual, structure_factor)


def solution(mesh):
    return jax.shard_map(
        body,
        mesh=mesh,
        in_specs=(P("row", "col"), P("depth", ("row", "col"))),
        out_specs=(P("row", ("col", "depth")), P("depth")),
        check_vma=False,
    )
```

profile of v0, /device:TPU:1, one launch (start us, length us, event | category | flops | bytes accessed | tf_op | source)
XLA Modules:
  0.0 711.8 jit_solution(17845553352122211983)
XLA Ops:
  7.2 0.0 all-reduce.2.cloned.1.call-start
  7.2 33.1 %all_gather.9 = bf16[128,2560]{0,1:T(8,128)(2,1)S(1)} all-gather(bf16[128,320]{0,1:T(8,128)(2,1)} %param.3), channel_id=1, replica_groups=mesh['row'=8,'col'=8,'depth'=2] {'col'}, dimensions={1}, use_global_device_ids=true | all-gather | bytes 737280 | tf_op jit(solution)/shard_map/all_gather | solution.py:17
  40.3 0.2 copy.17
  40.6 0.9 broadcast_select_fusion
  41.5 0.0 all-reduce.2.cloned.1.call-update
  41.5 0.0 reduce-scatter.4.cloned.1.call-start
  41.5 77.2 %all-reduce.2.cloned.1.call-done = bf16[128,2560]{1,0:T(8,128)(2,1)} async-done(((bf16[128,2560]{1,0:T(8,128)(2,1)}), bf16[128,2560]{1,0:T(8,128)(2,1)}) %all-reduce.2.cloned.1.call-update) | async-done | bytes 655376 | tf_op jit(solution)/shard_map/psum | solution.py:9
  118.7 6.9 multiply_reduce_fusion
  125.6 1.5 copy.22
  127.1 0.0 reduce-scatter.4.cloned.1.call-update
  127.1 0.0 all-gather.3.cloned.1.call-start
  127.1 42.3 %reduce-scatter.4.cloned.1.call-done = f32[320,128]{1,0:T(8,128)} async-done(((f32[2560,128]{1,0:T(8,128)}), f32[320,128]{1,0:T(8,128)}) %reduce-scatter.4.cloned.1.call-update) | async-done | bytes 163856
  169.5 1.6 bitcast_convert_fusion
  171.0 0.0 all-gather.3.cloned.1.call-update
  171.1 0.0 all-gather.5.cloned.1.call-start
  171.1 301.0 %all-gather.3.cloned.1.call-done = bf16[128,20480]{0,1:T(8,128)(2,1)} async-done(((bf16[128,320]{0,1:T(8,128)(2,1)}), bf16[128,20480]{0,1:T(8,128)(2,1)}) %all-gather.3.cloned.1.call-update) | async-done | bytes 5242896 | tf_op jit(solution)/shard_map/all_gather | solution.py:25
  472.2 2.9 copy.19
  475.1 0.9 constant_dynamic-slice_fusion
  476.0 0.0 all-gather.5.cloned.1.call-update
  476.1 148.3 %psum.15 = f32[128]{0:T(128)} all-reduce(f32[128]{0:T(128)S(1)} %get-tuple-element.4), channel_id=1, replica_groups=mesh['row'=8,'col'=8,'depth'=2] {'row','col'}, use_global_device_ids=true, to_apply=%region_3.4 | all-reduce | flops 128 | bytes 1024 | tf_op jit(solution)/shard_map/psum | solution.py:21
  624.3 74.7 %all_to_all.19 = bf16[128,2,1280]{0,2,1:T(8,128)(2,1)S(1)} all-to-all(bf16[128,2,1280]{0,2,1:T(8,128)(2,1)S(1)} %bitcast.19), channel_id=1, replica_groups=mesh['row'=8,'col'=8,'depth'=2] {'depth'}, dimensions={1} | all-to-all | bytes 1310720 | tf_op jit(solution)/shard_map/all_to_all | solution.py:34
  699.0 0.2 copy.20
  699.3 0.0 all-gather.5.cloned.1.call-done
  699.3 6.0 convolution_convert_fusion
Async XLA Ops:
  7.2 111.5 %all-reduce.2.cloned.1.call-start = ((), (), s32[]{:S(2)}) async-start(), calls=%async_computation.4 | async-start | bytes 1310720 | tf_op jit(solution)/shard_map/psum | solution.py:9
  41.5 128.0 %reduce-scatter.4.cloned.1.call-start = ((), (), s32[]{:S(2)}) async-start(), calls=%async_computation.5 | async-start | bytes 1474560
  127.1 345.1 %all-gather.3.cloned.1.call-start = ((), (), s32[]{:S(2)}) async-start(), calls=%async_computation.2 | async-start | bytes 5324800 | tf_op jit(solution)/shard_map/all_gather | solution.py:25
  171.1 528.3 %all-gather.5.cloned.1.call-start = ((), (), s32[]{:S(2)}) async-start(), calls=%async_computation.3 | async-start | bytes 1966080 | tf_op jit(solution)/shard_map/all_gather | solution.py:35
Sparse Core Ops, SparseCore 0:
  41.6 77.0 all-reduce.1
  127.2 42.2 reduce-scatter.3
  171.7 300.4 all-gather.2
  476.2 51.9 all-gather.4
where the time goes:
time: 712 us
  waiting for transfers between devices  421 us (59%)
  blocking collectives  256 us (36%)
  between operations  13.8 us (2%)
  matrix products  12.9 us (2%)
    all_gather x1, waiting for transfers between devices, body(): everything = lax.all_gather(dressed, ('row', 'col'), axis=1, tiled=True)  301 us
    psum x1, blocking collectives, body(): structure_factor = lax.psum(factor_part, ('row', 'col'))  148 us
    psum x1, waiting for transfers between devices, broadcast(): return lax.psum(jnp.where(mine, array, jnp.zeros_like(array)), axis)  77.2 us
    all_to_all x1, blocking collectives, body(): lax.all_to_all(dressed_cols, 'depth', split_axis=1, concat_axis=0, tiled=...  74.7 us
    unnamed x5, waiting for transfers between devices  42.4 us
    all_gather x1, blocking collectives, body(): vertex_rows = lax.all_gather(coulomb_vertex, 'col', axis=1, tiled=True)  33.1 us
  transfers between devices with their start and end apart: 4, of which 3 were waited for; matrix products, arithmetic and copies ran while one was open for 0% of the time, Pallas kernels for 0%

commit v1 on v0

--- a/solution.py
+++ b/solution.py
@@ -18,7 +18,7 @@
     vertex_cols = broadcast(vertex_rows, "row", col_index)
     dressing = jnp.dot(vertex_rows, amplitudes, preferred_element_type=jnp.float32)
     factor_part = jnp.sum(dressing * vertex_cols.astype(jnp.float32), axis=1)
-    structure_factor = lax.psum(factor_part, ("row", "col"))
+    structure_factor = lax.psum(lax.psum(factor_part, "col"), "row")
     dressed_term = dressing + on_diagonal * vertex_rows.astype(jnp.float32)
     dressed_part = lax.psum_scatter(dressed_term, "row", scatter_dimension=1, tiled=True)
     dressed = dressed_part.astype(jnp.bfloat16)

time: 712 us -> 576 us (0.81)
  blocking collectives: 256 us -> 120 us
    psum x1 -> x2, blocking collectives: 148 us -> 33.1 us  [body(): structure_factor = lax.psum(lax.psum(factor_part, 'col'), 'row')]
    all_to_all x1, blocking collectives: 74.7 us -> 54 us  [body(): lax.all_to_all(dressed_cols, 'depth', split_axis=1, concat_axis=0, tiled=...]
where the time goes in v1:
time: 576 us
  waiting for transfers between devices  421 us (73%)
  blocking collectives  120 us (21%)
  between operations  13.8 us (2%)
  matrix products  12.9 us (2%)
  local copies, waits for them, and re-layouts  5.82 us (1%)
    all_gather x1, waiting for transfers between devices, body(): everything = lax.all_gather(dressed, ('row', 'col'), axis=1, tiled=True)  301 us
    psum x1, waiting for transfers between devices, broadcast(): return lax.psum(jnp.where(mine, array, jnp.zeros_like(array)), axis)  77.2 us
    all_to_all x1, blocking collectives, body(): lax.all_to_all(dressed_cols, 'depth', split_axis=1, concat_axis=0, tiled=...  54 us
    unnamed x5, waiting for transfers between devices  42.4 us
    psum x2, blocking collectives, body(): structure_factor = lax.psum(lax.psum(factor_part, 'col'), 'row')  33.1 us
    all_gather x1, blocking collectives, body(): vertex_rows = lax.all_gather(coulomb_vertex, 'col', axis=1, tiled=True)  33.1 us
  transfers between devices with their start and end apart: 4, of which 3 were waited for; matrix products, arithmetic and copies ran while one was open for 0% of the time, Pallas kernels for 0%

profile of v1, /device:TPU:1, one launch (start us, length us, event | category | flops | bytes accessed | tf_op | source)
XLA Modules:
  0.0 575.9 jit_solution(15061622711367103999)
XLA Ops:
  7.2 0.0 all-reduce.2.cloned.1.call-start
  7.2 33.1 %all_gather.9 = bf16[128,2560]{0,1:T(8,128)(2,1)S(1)} all-gather(bf16[128,320]{0,1:T(8,128)(2,1)} %param.3), channel_id=1, replica_groups=mesh['row'=8,'col'=8,'depth'=2] {'col'}, dimensions={1}, use_global_device_ids=true | all-gather | bytes 737280 | tf_op jit(solution)/shard_map/all_gather | solution.py:17
  40.3 0.2 copy.17
  40.6 0.9 broadcast_select_fusion
  41.5 0.0 all-reduce.2.cloned.1.call-update
  41.5 0.0 reduce-scatter.4.cloned.1.call-start
  41.5 77.2 %all-reduce.2.cloned.1.call-done = bf16[128,2560]{1,0:T(8,128)(2,1)} async-done(((bf16[128,2560]{1,0:T(8,128)(2,1)}), bf16[128,2560]{1,0:T(8,128)(2,1)}) %all-reduce.2.cloned.1.call-update) | async-done | bytes 655376 | tf_op jit(solution)/shard_map/psum | solution.py:9
  118.7 6.9 %multiply_reduce_fusion = (f32[128]{0:T(128)S(1)}, f32[128,2560]{1,0:T(8,128)S(1)}) fusion(bf16[128,2560]{1,0:T(8,128)(2,1)} %all-reduce.2.cloned.1.call-done, bf16[128,2560]{1,0:T(8,128)(2,1)S(1)} %copy.17, f32[]{:T(128)S(6)} %convert_element_type.15, bf16[128,2560]{0,1:T(8,128)(2,1)S(1)} %all_gather.9, bf16[2560,2560]{1,0:T(8,128)(2,1)} %param.2), kind=kOutput, calls=%fused_computation.1 | convolution fusion | flops 1679687552 | bytes 16384516 | tf_op jit(solution)/shard_map/dot_general | solution.py:19
  125.6 1.5 copy.22
  127.1 0.0 reduce-scatter.4.cloned.1.call-update
  127.1 0.0 all-gather.3.cloned.1.call-start
  127.1 42.3 %reduce-scatter.4.cloned.1.call-done = f32[320,128]{1,0:T(8,128)} async-done(((f32[2560,128]{1,0:T(8,128)}), f32[320,128]{1,0:T(8,128)}) %reduce-scatter.4.cloned.1.call-update) | async-done | bytes 163856
  169.5 1.6 bitcast_convert_fusion
  171.0 0.0 all-gather.3.cloned.1.call-update
  171.1 0.0 all-gather.5.cloned.1.call-start
  171.1 301.0 %all-gather.3.cloned.1.call-done = bf16[128,20480]{0,1:T(8,128)(2,1)} async-done(((bf16[128,320]{0,1:T(8,128)(2,1)}), bf16[128,20480]{0,1:T(8,128)(2,1)}) %all-gather.3.cloned.1.call-update) | async-done | bytes 5242896 | tf_op jit(solution)/shard_map/all_gather | solution.py:25
  472.2 2.9 copy.19
  475.1 0.9 constant_dynamic-slice_fusion
  476.0 0.0 all-gather.5.cloned.1.call-update
  476.1 16.4 %psum.22 = f32[128]{0:T(128)S(1)} all-reduce(f32[128]{0:T(128)S(1)} %get-tuple-element.4), channel_id=1, replica_groups=mesh['row'=8,'col'=8,'depth'=2] {'col'}, use_global_device_ids=true, to_apply=%region_3.4 | all-reduce | flops 128 | bytes 1024 | tf_op jit(solution)/shard_map/psum | solution.py:21
  492.4 16.7 %psum.23 = f32[128]{0:T(128)} all-reduce(f32[128]{0:T(128)S(1)} %psum.22), channel_id=1, replica_groups=mesh['row'=8,'col'=8,'depth'=2] {'row'}, use_global_device_ids=true, to_apply=%region_4.5 | all-reduce | flops 128 | bytes 1024 | tf_op jit(solution)/shard_map/psum | solution.py:21
  509.2 54.0 %all_to_all.19 = bf16[128,2,1280]{0,2,1:T(8,128)(2,1)S(1)} all-to-all(bf16[128,2,1280]{0,2,1:T(8,128)(2,1)S(1)} %bitcast.19), channel_id=1, replica_groups=mesh['row'=8,'col'=8,'depth'=2] {'depth'}, dimensions={1} | all-to-all | bytes 1310720 | tf_op jit(solution)/shard_map/all_to_all | solution.py:34
  563.1 0.2 copy.20
  563.4 0.0 all-gather.5.cloned.1.call-done
  563.4 6.0 %convolution_convert_fusion = bf16[2560,1280]{1,0:T(8,128)(2,1)} fusion(bf16[256,2560]{0,1:T(8,128)(2,1)} %all-gather.5.cloned.1.call-done, bf16[256,1280]{1,0:T(8,128)(2,1)S(1)} %bitcast.17), kind=kOutput, calls=%fused_computation | convolution fusion | flops 1680998400 | bytes 8519680 | tf_op jit(solution)/shard_map/dot_general | solution.py:36
Async XLA Ops:
  7.2 111.5 %all-reduce.2.cloned.1.call-start = ((), (), s32[]{:S(2)}) async-start(), calls=%async_computation.4 | async-start | bytes 1310720 | tf_op jit(solution)/shard_map/psum | solution.py:9
  41.5 128.0 %reduce-scatter.4.cloned.1.call-start = ((), (), s32[]{:S(2)}) async-start(), calls=%async_computation.5 | async-start | bytes 1474560
  127.1 345.1 %all-gather.3.cloned.1.call-start = ((), (), s32[]{:S(2)}) async-start(), calls=%async_computation.2 | async-start | bytes 5324800 | tf_op jit(solution)/shard_map/all_gather | solution.py:25
  171.1 392.3 %all-gather.5.cloned.1.call-start = ((), (), s32[]{:S(2)}) async-start(), calls=%async_computation.3 | async-start | bytes 1966080 | tf_op jit(solution)/shard_map/all_gather | solution.py:35
Sparse Core Ops, SparseCore 0:
  41.6 77.0 all-reduce.1
  127.2 42.2 reduce-scatter.3
  171.7 300.4 all-gather.2
  476.2 51.8 all-gather.4
